TPU v7x, 128 devices: a whole 4x4x4 slice. The times are simulated.
128 devices in a mesh: row: 4 (over y), col: 32 (over x, z, core).
Axes of the slice: x: 4, y: 4, z: 4, core: 2. Of those that a mesh axis runs over, the one named last changes fastest.
Arguments:
- frontal: bfloat16 [16384, 49152], P('row', 'col')
- sample_cols: bfloat16 [49152, 64], P(('col', 'row')), may hold values from -6 to 6
- leaf_first: int32 [256], replicated, may hold values from 0 to 16352, as said below
- leaf_owner: int32 [256], replicated, may hold values from 0 to 31, as said below
- skeleton: int32 [256, 16], replicated, may hold values from 0 to 16383, as said below
Outputs:
- owner_samples: float32 [256, 8192], P('row', 'col')
- interp: float32 [64, 8192], P('row', 'col')
- worst: float32 [1], replicated
Inputs may be any that keep to these rules, and one draw needn't show every extreme that they name: `leaf_first`: leaves are consecutive and ascending; the first leaf of row group g starts at g * 4096; each row group has 64 leaves whose sizes are 1 to 5 times 32, in 16 runs of four consecutive leaves of together 256 rows. `leaf_owner`: each run of four leaves is owned by at most two devices of the group; the leaves one device owns in its group hold at most 256 rows and number at most 4; in every row group some device reaches both. Each leaf's skeleton rows are 16 distinct rows of that leaf, ascending.
All inputs are finite; a program needn't handle non-finite values.
Results may differ from a plain program's by a relative error of at most 0.0003.
Values may be sent and summed in bfloat16 or wider, within the bound.
A program may use at most 64 MiB of HBM per device.

v0:
```python
import jax
import jax.numpy as jnp
from jax import lax
from jax.sharding import PartitionSpec as P

LEAF_MOST = 4


def leaf_index(values, leaf_first):
    return jnp.sum((leaf_first[None, :] <= values[:, None]).astype(jnp.int32), axis=1) - 1


def local(frontal, sample_cols, leaf_first, leaf_owner, skeleton):
    highest = lax.Precision.HIGHEST
    group_rows, width = frontal.shape
    samples_count = sample_cols.shape[1]
    skel_count = skeleton.shape[1]
    leaves = leaf_first.shape[0]
    n_col = lax.axis_size("col")
    n_row = lax.axis_size("row")
    per_group = leaves // n_row
    total_rows = group_rows * n_row
    share_rows = group_rows // n_col
    capacity = 2 * share_rows
    row_pos = lax.axis_index("row")
    col_pos = lax.axis_index("col")
    rows = row_pos * group_rows + jnp.arange(group_rows, dtype=jnp.int32)
    row_leaf = leaf_index(rows, leaf_first)
    zero_entry = jnp.zeros((), frontal.dtype)
    piece = lax.all_gather(sample_cols, "row", axis=0, tiled=True)
    span = piece.shape[0]
    cols = col_pos * width + jnp.arange(span, dtype=jnp.int32)
    col_leaf = leaf_index(cols, leaf_first)
    same = (row_leaf[:, None] == col_leaf[None, :]) & (cols[None, :] < total_rows)
    kept = jnp.where(same, zero_entry, frontal)
    partial_value = jnp.dot(kept, piece, preferred_element_type=jnp.float32)
    ends = jnp.concatenate([leaf_first[1:], jnp.full((1,), total_rows, jnp.int32)])
    sizes = ends - leaf_first
    leaf_ids = jnp.arange(leaves, dtype=jnp.int32)
    group_of = leaf_ids // per_group
    own_hot = (leaf_owner[:, None] == jnp.arange(n_col, dtype=jnp.int32)[None, :]).astype(jnp.int32)
    weighted = (own_hot * sizes[:, None]).reshape(n_row, per_group, n_col)
    before = (jnp.cumsum(weighted, axis=1) - weighted).reshape(leaves, n_col)
    offset = jnp.sum(before * own_hot, axis=1)
    counted = own_hot.reshape(n_row, per_group, n_col)
    earlier = (jnp.cumsum(counted, axis=1) - counted).reshape(leaves, n_col)
    rank = jnp.sum(earlier * own_hot, axis=1)
    owned = (leaf_owner == col_pos) & (group_of == row_pos)
    slots = jnp.arange(capacity, dtype=jnp.int32)
    slot_hit = (
        owned[None, :]
        & (offset[None, :] <= slots[:, None])
        & (slots[:, None] < (offset + sizes)[None, :])
    )
    slot_hit_int = slot_hit.astype(jnp.int32)
    valid = jnp.any(slot_hit, axis=1)
    local_row = (
        jnp.sum(slot_hit_int * (leaf_first[None, :] + slots[:, None] - offset[None, :]), axis=1)
        - row_pos * group_rows
    )
    local_row = jnp.clip(local_row, 0, group_rows - 1)
    valid_float = valid[:, None].astype(jnp.float32)
    summed = lax.psum(partial_value, "col")
    mine = jnp.take(summed, local_row, axis=0) * valid_float
    select = owned[None, :] & (rank[None, :] == jnp.arange(LEAF_MOST, dtype=jnp.int32)[:, None])
    select_int = select.astype(jnp.int32)
    present = jnp.any(select, axis=1).astype(jnp.float32)
    skel_slot = jnp.sum(
        select_int[:, :, None] * (offset[:, None] + skeleton - leaf_first[:, None])[None, :, :],
        axis=1,
    )
    skel_slot = jnp.clip(skel_slot, 0, capacity - 1)
    picked = jnp.take(mine, skel_slot.reshape(-1), axis=0).reshape(
        LEAF_MOST, skel_count, samples_count
    )
    picked = picked * present[:, None, None]
    identity = jnp.eye(skel_count, dtype=jnp.float32)
    gram = jnp.einsum("kjp,kip->kji", picked, picked, precision=highest)
    gram = gram + (1.0 - present)[:, None, None] * identity[None, :, :]
    factor = jnp.linalg.cholesky(gram)
    inverse = jax.vmap(lambda lower: jax.scipy.linalg.cho_solve((lower, True), identity))(factor)
    slot_rank = jnp.sum(slot_hit_int * rank[None, :], axis=1)
    slot_pick = (
        (slot_rank[:, None] == jnp.arange(LEAF_MOST, dtype=jnp.int32)[None, :]) & valid[:, None]
    ).astype(jnp.float32)
    project = jnp.einsum("sp,kjp->skj", mine, picked, precision=highest)
    coeff_all = jnp.einsum("skj,kji->ski", project, inverse, precision=highest)
    coeff = jnp.sum(coeff_all * slot_pick[:, :, None], axis=1)
    rebuilt_all = jnp.einsum("ski,kip->skp", coeff_all, picked, precision=highest)
    rebuilt = jnp.sum(rebuilt_all * slot_pick[:, :, None], axis=1)
    resid = mine - rebuilt
    err = jnp.sum(slot_pick * jnp.sum(resid * resid, axis=1)[:, None], axis=0)
    norm = jnp.sum(slot_pick * jnp.sum(mine * mine, axis=1)[:, None], axis=0)
    ratio = jnp.sqrt(err) / jnp.sqrt(norm + 1e-06)
    local_worst = jnp.max(jnp.where(present > 0.5, ratio, 0.0)).reshape(1)
    worst = lax.pmax(local_worst, ("row", "col"))
    return (mine.T, coeff.T, worst)


def solution(mesh):
    return jax.shard_map(
        local,
        mesh=mesh,
        in_specs=(P("row", "col"), P(("col", "row"), None), P(), P(), P()),
        out_specs=(P("row", "col"), P("row", "col"), P()),
        check_vma=False,
    )
```

profile of v0, /device:TPU:1, one launch (start us, length us, event | category | flops | bytes accessed | tf_op | source)
XLA Modules:
  0.0 230.8 jit_solution(219416975980167111)
XLA Ops:
  7.2 0.0 all-reduce.2.cloned.1.call-start
  7.2 10.9 %all_gather.3 = bf16[1536,64]{0,1:T(8,128)(2,1)S(1)} all-gather(bf16[384,64]{0,1:T(8,128)(2,1)} %param.6), channel_id=1, replica_groups=mesh['row'=4,'col'=32] {'row'}, dimensions={0}, use_global_device_ids=true | all-gather | bytes 245760 | tf_op jit(solution)/shard_map/all_gather | solution.py:30
  18.2 1.2 convert_reduce_fusion.1
  19.4 2.0 convert_reduce_fusion
  21.4 0.0 copy-start
  21.4 0.0 copy-start.2
  21.4 0.0 copy-start.1
  21.4 7.9 %fusion = f32[4096,64]{0,1:T(8,128)} fusion(bf16[1536,64]{0,1:T(8,128)(2,1)S(1)} %all_gather.3, bf16[4096,1536]{1,0:T(8,128)(2,1)} %param.5, s32[1536]{0:T(1024)S(1)} %broadcast_add_fusion.1, s32[4096]{0:T(1024)S(1)} %broadcast_add_fusion, pred[1536]{0:T(1024)(128)(4,1)S(1)} %broadcast_compare_fusion), kind=kOutput, calls=%fused_computation.3 | convolution fusion | flops 824180736 | bytes 13852160 | tf_op jit(solution)/shard_map/dot_general | solution.py:36
  29.3 0.0 all-reduce.2.cloned.1.call-update
  29.3 0.0 copy-done
  29.3 0.1 slice.21
  29.4 0.0 copy-done.2
  29.4 0.1 eq.93
  29.5 0.1 fusion.10
  29.6 0.1 add_subtract_fusion.1
  29.7 0.1 mul.125
  29.8 0.1 fusion.11
  29.9 0.1 reduce_window_sum.18
  30.0 0.1 reduce_window_sum.17
  30.2 0.3 select_reduce_fusion.2
  30.5 0.1 le.64
  30.6 0.1 eq.100
  30.7 0.1 fusion.19
  30.8 0.2 select_reduce_fusion
  31.1 0.1 fusion.33
  31.3 0.0 copy-done.1
  31.3 0.1 multiply_reduce_fusion.3
  31.5 0.1 min.25
  31.6 108.0 %all-reduce.2.cloned.1.call-done = f32[4096,64]{0,1:T(8,128)} async-done(((f32[4096,64]{0,1:T(8,128)}), f32[4096,64]{0,1:T(8,128)}) %all-reduce.2.cloned.1.call-update) | async-done | bytes 1048592 | tf_op jit(solution)/shard_map/psum | solution.py:63
  139.6 1.8 copy.23
  141.4 0.7 gather_fusion
  142.1 0.1 fusion.48
  142.3 0.1 select_multiply_fusion
  142.4 0.6 gather_fusion.1
  143.0 0.3 fusion.18
  143.3 0.3 fusion.8
  143.6 0.7 copy.28
  144.3 0.1 copy.24
  144.4 0.1 fusion.17
  144.5 5.9 %custom-call.11 = f32[4,16,16]{2,1,0:T(8,128)S(1)} custom-call(f32[4,16,16]{2,1,0:T(8,128)S(1)} %fusion.17), custom_call_target="Cholesky" | custom-call | tf_op jit(solution)/shard_map/jit(cholesky)/cholesky | solution.py:80
  150.4 0.1 compare_reduce_fusion
  150.5 0.1 select_bitcast_fusion
  150.6 4.9 %custom-call.12 = f32[4,1,16,16]{2,3,1,0:T(8,128)S(1)} custom-call(f32[4,1,16,16]{3,2,1,0:T(8,128)S(1)} %select_bitcast_fusion), custom_call_target="InvertDiagBlocksLowerTriangular" | custom-call | tf_op jit(solution)/shard_map/vmap(jit(_cho_solve))/triangular_solve | solution.py:81
  155.5 0.3 fusion.14
  155.8 0.2 fusion.12
  156.0 0.8 multiply_reduce_fusion.2
  156.8 0.5 fusion.5
  157.3 0.1 copy.27
  157.4 0.3 multiply_reduce_fusion.1
  157.7 0.2 select_reduce_fusion.6
  157.8 0.6 fusion.36
  158.4 65.5 %pmax.7 = f32[1]{0:T(128)} all-reduce(f32[1]{0:T(128)} %bitcast.12), channel_id=1, replica_groups=mesh['row'=4,'col'=32] {'row','col'}, use_global_device_ids=true, to_apply=%region_21.22 | all-reduce | flops 1 | bytes 8 | tf_op jit(solution)/shard_map/pmax | solution.py:96
  (23 shorter events, 0.2 us)
Async XLA Ops:
  7.2 132.4 %all-reduce.2.cloned.1.call-start = ((), (), s32[]{:S(2)}) async-start(), calls=%async_computation | async-start | bytes 2097152 | tf_op jit(solution)/shard_map/psum | solution.py:63
  21.4 7.9 %copy-start = (s32[256]{0:T(256)S(1)}, s32[256]{0:T(256)}, u32[]{:S(2)}) copy-start(s32[256]{0:T(256)} %param.7) | copy-start | bytes 3076
  21.4 8.0 %copy-start.2 = (s32[256]{0:T(256)S(1)}, s32[256]{0:T(256)}, u32[]{:S(2)}) copy-start(s32[256]{0:T(256)} %param.8) | copy-start | bytes 3076
  21.4 9.9 %copy-start.1 = (s32[256,16]{0,1:T(8,128)S(1)}, s32[256,16]{0,1:T(8,128)}, u32[]{:S(2)}) copy-start(s32[256,16]{0,1:T(8,128)} %param.9) | copy-start | bytes 49156
Sparse Core Ops, SparseCore 0:
  29.4 110.0 all-reduce.1
where the time goes:
time: 231 us
  waiting for transfers between devices  108 us (47%)
  blocking collectives  76.5 us (33%)
  other arithmetic  17.2 us (7%)
  between operations  14.3 us (6%)
  matrix products  10.3 us (4%)
  local copies, waits for them, and re-layouts  4.54 us (2%)
    psum x1, waiting for transfers between devices, local(): summed = lax.psum(partial_value, 'col')  108 us
    pmax x1, blocking collectives, local(): worst = lax.pmax(local_worst, ('row', 'col'))  65.5 us
    all_gather x1, blocking collectives, local(): piece = lax.all_gather(sample_cols, 'row', axis=0, tiled=True)  10.9 us
    dot_general x1, matrix products, local(): partial_value = jnp.dot(kept, piece, preferred_element_type=jnp.float32)  7.88 us
    another operation x4, other arithmetic, local(): factor = jnp.linalg.cholesky(gram)  6.03 us
    another operation x3, other arithmetic, local(): jax.scipy.linalg.cho_solve((lower, True), identity)  5 us
  transfers between devices with their start and end apart: 1, of which 1 were waited for; matrix products, arithmetic and copies ran while one was open for 1% of the time, Pallas kernels for 0%

commit v1 on v0

--- a/solution.py
+++ b/solution.py
@@ -4,6 +4,14 @@
 from jax.sharding import PartitionSpec as P
 
 LEAF_MOST = 4
+
+
+def sum_by_hops(array, mesh_axis):
+    size, acc = (lax.axis_size(mesh_axis), array)
+    for reach in [1 << k for k in range(size.bit_length() - 1)]:
+        swap = [(i, i ^ reach) for i in range(size)]
+        acc = acc + lax.ppermute(acc, mesh_axis, swap)
+    return acc
 
 
 def leaf_index(values, leaf_first):
@@ -60,7 +68,7 @@
     )
     local_row = jnp.clip(local_row, 0, group_rows - 1)
     valid_float = valid[:, None].astype(jnp.float32)
-    summed = lax.psum(partial_value, "col")
+    summed = sum_by_hops(partial_value, "col")
     mine = jnp.take(summed, local_row, axis=0) * valid_float
     select = owned[None, :] & (rank[None, :] == jnp.arange(LEAF_MOST, dtype=jnp.int32)[:, None])
     select_int = select.astype(jnp.int32)

time: 231 us -> 211 us (0.913)
  waiting for transfers between devices: 108 us -> 88 us
  between operations: 14.3 us -> 0.9 us
  starting transfers between devices: 0.04 us -> 12.7 us
    psum x1 -> x0, waiting for transfers between devices: 108 us -> none  [local(): summed = lax.psum(partial_value, 'col')]
    ppermute x0 -> x5, waiting for transfers between devices: none -> 88 us  [sum_by_hops(): acc = acc + lax.ppermute(acc, mesh_axis, swap)]
    ppermute x0 -> x5, starting transfers between devices: none -> 12.7 us  [sum_by_hops(): acc = acc + lax.ppermute(acc, mesh_axis, swap)]
  transfers between devices with their start and end apart: 1 -> 5, of which waited for: 1 -> 5; matrix products, arithmetic and copies ran while one was open for 1% -> 1% of each run, Pallas kernels for 0% -> 0%
where the time goes in v1:
time: 211 us
  waiting for transfers between devices  88 us (42%)
  blocking collectives  78.4 us (37%)
  other arithmetic  17.8 us (8%)
  starting transfers between devices  12.7 us (6%)
  matrix products  9.86 us (5%)
  local copies, waits for them, and re-layouts  3.3 us (2%)
    ppermute x5, waiting for transfers between devices, sum_by_hops(): acc = acc + lax.ppermute(acc, mesh_axis, swap)  88 us
    pmax x1, blocking collectives, local(): worst = lax.pmax(local_worst, ('row', 'col'))  67.5 us
    ppermute x5, starting transfers between devices, sum_by_hops(): acc = acc + lax.ppermute(acc, mesh_axis, swap)  12.7 us
    all_gather x1, blocking collectives, local(): piece = lax.all_gather(sample_cols, 'row', axis=0, tiled=True)  10.9 us
    dot_general x1, matrix products, local(): partial_value = jnp.dot(kept, piece, preferred_element_type=jnp.float32)  7.47 us
    another operation x4, other arithmetic, local(): factor = jnp.linalg.cholesky(gram)  6.03 us
    another operation x3, other arithmetic, local(): jax.scipy.linalg.cho_solve((lower, True), identity)  5 us
  transfers between devices with their start and end apart: 5, of which 5 were waited for; matrix products, arithmetic and copies ran while one was open for 1% of the time, Pallas kernels for 0%

profile of v1, /device:TPU:1, one launch (start us, length us, event | category | flops | bytes accessed | tf_op | source)
XLA Modules:
  0.0 211.1 jit_solution(13716313358438469923)
XLA Ops:
  0.7 2.0 convert_reduce_fusion
  2.7 1.2 convert_reduce_fusion.1
  3.9 10.9 %all_gather.3 = bf16[1536,64]{0,1:T(8,128)(2,1)S(1)} all-gather(bf16[384,64]{0,1:T(8,128)(2,1)} %param.6), channel_id=1, replica_groups=mesh['row'=4,'col'=32] {'row'}, dimensions={0}, use_global_device_ids=true | all-gather | bytes 245760 | tf_op jit(solution)/shard_map/all_gather | solution.py:38
  14.8 0.0 copy-start
  14.8 0.0 copy-start.2
  14.8 7.5 %fusion = f32[4096,64]{0,1:T(8,128)S(1)} fusion(bf16[1536,64]{0,1:T(8,128)(2,1)S(1)} %all_gather.3, bf16[4096,1536]{1,0:T(8,128)(2,1)} %param.5, s32[1536]{0:T(1024)S(1)} %broadcast_add_fusion.1, s32[4096]{0:T(1024)S(1)} %broadcast_add_fusion, pred[1536]{0:T(1024)(128)(4,1)S(1)} %broadcast_compare_fusion), kind=kOutput, calls=%fused_computation.3 | convolution fusion | flops 824180736 | bytes 13852160 | tf_op jit(solution)/shard_map/dot_general | solution.py:44
  22.3 0.0 copy-start.1
  22.3 3.6 %collective-permute-start = (f32[4096,64]{0,1:T(8,128)S(1)}, f32[4096,64]{0,1:T(8,128)S(1)}, u32[]{:S(2)}, u32[]{:S(2)}) collective-permute-start(f32[4096,64]{0,1:T(8,128)S(1)} %fusion), channel_id=1, source_target_pairs={{0,1},{1,0},{2,3},{3,2},{4,5},{5,4},{6,7},{7,6},{8,9},{9,8},{10,11... | collective-permute-start | bytes 3145736 | tf_op jit(solution)/shard_map/ppermute | solution.py:13
  25.9 2.3 %collective-permute-done = f32[4096,64]{0,1:T(8,128)S(1)} collective-permute-done((f32[4096,64]{0,1:T(8,128)S(1)}, f32[4096,64]{0,1:T(8,128)S(1)}, u32[]{:S(2)}, u32[]{:S(2)}) %collective-permute-start) | collective-permute-done | bytes 1048608 | tf_op jit(solution)/shard_map/ppermute | solution.py:13
  28.1 0.2 add.148
  28.3 1.7 collective-permute-start.1
  30.0 0.0 copy-done
  30.0 0.1 slice.21
  30.1 0.1 add_subtract_fusion.1
  30.2 0.1 mul.125
  30.3 0.0 copy-done.2
  30.3 0.1 eq.93
  30.4 0.1 fusion.11
  30.5 0.1 reduce_window_sum.17
  30.6 22.5 %collective-permute-done.1 = f32[4096,64]{0,1:T(8,128)S(1)} collective-permute-done((f32[4096,64]{0,1:T(8,128)S(1)}, f32[4096,64]{0,1:T(8,128)S(1)}, u32[]{:S(2)}, u32[]{:S(2)}) %collective-permute-start.1) | collective-permute-done | bytes 1048608 | tf_op jit(solution)/shard_map/ppermute | solution.py:13
  53.1 0.1 add.149
  53.2 3.3 %collective-permute-start.2 = (f32[4096,64]{0,1:T(8,128)S(1)}, f32[4096,64]{0,1:T(8,128)S(1)}, u32[]{:S(2)}, u32[]{:S(2)}) collective-permute-start(f32[4096,64]{0,1:T(8,128)S(1)} %add.149), channel_id=1, source_target_pairs={{0,4},{1,5},{2,6},{3,7},{4,0},{5,1},{6,2},{7,3},{8,12},{9,13},{10,... | collective-permute-start | bytes 3145736 | tf_op jit(solution)/shard_map/ppermute | solution.py:13
  56.5 0.1 fusion.10
  56.6 0.1 reduce_window_sum.18
  56.8 0.3 select_reduce_fusion.2
  57.1 0.1 le.64
  57.2 0.1 eq.100
  57.3 0.1 fusion.33
  57.4 0.0 copy-done.1
  57.4 0.1 multiply_reduce_fusion.3
  57.6 21.3 %collective-permute-done.2 = f32[4096,64]{0,1:T(8,128)S(1)} collective-permute-done((f32[4096,64]{0,1:T(8,128)S(1)}, f32[4096,64]{0,1:T(8,128)S(1)}, u32[]{:S(2)}, u32[]{:S(2)}) %collective-permute-start.2) | collective-permute-done | bytes 1048608 | tf_op jit(solution)/shard_map/ppermute | solution.py:13
  78.8 0.1 add.150
  78.9 1.3 collective-permute-start.3
  80.2 0.1 min.25
  80.3 0.1 fusion.19
  80.5 0.2 select_reduce_fusion
  80.8 21.2 %collective-permute-done.3 = f32[4096,64]{0,1:T(8,128)S(1)} collective-permute-done((f32[4096,64]{0,1:T(8,128)S(1)}, f32[4096,64]{0,1:T(8,128)S(1)}, u32[]{:S(2)}, u32[]{:S(2)}) %collective-permute-start.3) | collective-permute-done | bytes 1048608 | tf_op jit(solution)/shard_map/ppermute | solution.py:13
  101.9 0.1 add.151
  102.1 2.8 %collective-permute-start.4 = (f32[4096,64]{0,1:T(8,128)S(1)}, f32[4096,64]{0,1:T(8,128)S(1)}, u32[]{:S(2)}, u32[]{:S(2)}) collective-permute-start(f32[4096,64]{0,1:T(8,128)S(1)} %add.151), channel_id=1, source_target_pairs={{0,16},{1,17},{2,18},{3,19},{4,20},{5,21},{6,22},{7,23},{8,24},{9,... | collective-permute-start | bytes 3145736 | tf_op jit(solution)/shard_map/ppermute | solution.py:13
  105.0 20.8 %collective-permute-done.4 = f32[4096,64]{0,1:T(8,128)S(1)} collective-permute-done((f32[4096,64]{0,1:T(8,128)S(1)}, f32[4096,64]{0,1:T(8,128)S(1)}, u32[]{:S(2)}, u32[]{:S(2)}) %collective-permute-start.4) | collective-permute-done | bytes 1048608 | tf_op jit(solution)/shard_map/ppermute | solution.py:13
  125.8 0.1 add.152
  125.9 0.6 copy.23
  126.5 0.7 gather_fusion
  127.3 0.1 select_multiply_fusion
  127.4 0.6 gather_fusion.1
  128.0 0.3 fusion.8
  128.3 0.3 fusion.18
  128.6 0.1 fusion.48
  128.7 0.1 copy.24
  128.8 0.1 fusion.17
  128.9 5.9 %custom-call.11 = f32[4,16,16]{2,1,0:T(8,128)S(1)} custom-call(f32[4,16,16]{2,1,0:T(8,128)S(1)} %fusion.17), custom_call_target="Cholesky" | custom-call | tf_op jit(solution)/shard_map/jit(cholesky)/cholesky | solution.py:88
  134.8 0.1 compare_reduce_fusion
  134.9 0.1 select_bitcast_fusion
  135.0 4.9 %custom-call.12 = f32[4,1,16,16]{2,3,1,0:T(8,128)S(1)} custom-call(f32[4,1,16,16]{3,2,1,0:T(8,128)S(1)} %select_bitcast_fusion), custom_call_target="InvertDiagBlocksLowerTriangular" | custom-call | tf_op jit(solution)/shard_map/vmap(jit(_cho_solve))/triangular_solve | solution.py:89
  139.9 0.3 fusion.14
  140.2 0.2 fusion.12
  140.4 0.8 multiply_reduce_fusion.2
  141.2 0.5 fusion.5
  141.7 0.1 copy.27
  141.8 0.3 multiply_reduce_fusion.1
  142.1 0.2 select_reduce_fusion.6
  142.2 0.6 fusion.36
  142.9 67.5 %pmax.7 = f32[1]{0:T(128)} all-reduce(f32[1]{0:T(128)} %bitcast.12), channel_id=1, replica_groups=mesh['row'=4,'col'=32] {'row','col'}, use_global_device_ids=true, to_apply=%region_20.21 | all-reduce | flops 1 | bytes 8 | tf_op jit(solution)/shard_map/pmax | solution.py:104
  210.4 0.7 copy.28
  (23 shorter events, 0.2 us)
Async XLA Ops:
  14.8 15.2 %copy-start = (s32[256]{0:T(256)S(1)}, s32[256]{0:T(256)}, u32[]{:S(2)}) copy-start(s32[256]{0:T(256)} %param.7) | copy-start | bytes 3076
  14.8 15.5 %copy-start.2 = (s32[256]{0:T(256)S(1)}, s32[256]{0:T(256)}, u32[]{:S(2)}) copy-start(s32[256]{0:T(256)} %param.8) | copy-start | bytes 3076
  22.3 35.1 %copy-start.1 = (s32[256,16]{0,1:T(8,128)S(1)}, s32[256,16]{0,1:T(8,128)}, u32[]{:S(2)}) copy-start(s32[256,16]{0,1:T(8,128)} %param.9) | copy-start | bytes 49156
  22.3 5.9 %collective-permute-start = (f32[4096,64]{0,1:T(8,128)S(1)}, f32[4096,64]{0,1:T(8,128)S(1)}, u32[]{:S(2)}, u32[]{:S(2)}) collective-permute-start(f32[4096,64]{0,1:T(8,128)S(1)} %fusion), channel_id=1, source_target_pairs={{0,1},{1,0},{2,3},{3,2},{4,5},{5,4},{6,7},{7,6},{8,9},{9,8},{10,11... | collective-permute-start | bytes 3145736 | tf_op jit(solution)/shard_map/ppermute | solution.py:13
  28.3 24.8 %collective-permute-start.1 = (f32[4096,64]{0,1:T(8,128)S(1)}, f32[4096,64]{0,1:T(8,128)S(1)}, u32[]{:S(2)}, u32[]{:S(2)}) collective-permute-start(f32[4096,64]{0,1:T(8,128)S(1)} %add.148), channel_id=1, source_target_pairs={{0,2},{1,3},{2,0},{3,1},{4,6},{5,7},{6,4},{7,5},{8,10},{9,11},{10,... | collective-permute-start | bytes 3145736 | tf_op jit(solution)/shard_map/ppermute | solution.py:13
  53.2 25.6 %collective-permute-start.2 = (f32[4096,64]{0,1:T(8,128)S(1)}, f32[4096,64]{0,1:T(8,128)S(1)}, u32[]{:S(2)}, u32[]{:S(2)}) collective-permute-start(f32[4096,64]{0,1:T(8,128)S(1)} %add.149), channel_id=1, source_target_pairs={{0,4},{1,5},{2,6},{3,7},{4,0},{5,1},{6,2},{7,3},{8,12},{9,13},{10,... | collective-permute-start | bytes 3145736 | tf_op jit(solution)/shard_map/ppermute | solution.py:13
  78.9 23.0 %collective-permute-start.3 = (f32[4096,64]{0,1:T(8,128)S(1)}, f32[4096,64]{0,1:T(8,128)S(1)}, u32[]{:S(2)}, u32[]{:S(2)}) collective-permute-start(f32[4096,64]{0,1:T(8,128)S(1)} %add.150), channel_id=1, source_target_pairs={{0,8},{1,9},{2,10},{3,11},{4,12},{5,13},{6,14},{7,15},{8,0},{9,1},... | collective-permute-start | bytes 3145736 | tf_op jit(solution)/shard_map/ppermute | solution.py:13
  102.1 23.8 %collective-permute-start.4 = (f32[4096,64]{0,1:T(8,128)S(1)}, f32[4096,64]{0,1:T(8,128)S(1)}, u32[]{:S(2)}, u32[]{:S(2)}) collective-permute-start(f32[4096,64]{0,1:T(8,128)S(1)} %add.151), channel_id=1, source_target_pairs={{0,16},{1,17},{2,18},{3,19},{4,20},{5,21},{6,22},{7,23},{8,24},{9,... | collective-permute-start | bytes 3145736 | tf_op jit(solution)/shard_map/ppermute | solution.py:13
